TPU v7x, 32 devices: a whole 2x2x4 slice. The times are simulated.
32 devices in a mesh: fsdp: 4 (over y, x), heads: 2 (over core), tensor: 4 (over z).
Axes of the slice: x: 2, y: 2, z: 4, core: 2. Of those that a mesh axis runs over, the one named last changes fastest.
Arguments:
- inputs: float32 [32, 729, 1152], P(('fsdp', 'heads', 'tensor')), may hold values from -6 to 6
- cotangent: float32 [32, 729, 1152], P(('fsdp', 'heads', 'tensor')), may hold values from -6 to 6
- image_adapter_index: int32 [32], replicated, may hold values from 0 to 7
- first_norm_gain: float32 [1152], replicated, may hold values from 0.5 to 1.5
- first_norm_bias: float32 [1152], replicated, may hold values from -3 to 3
- second_norm_gain: float32 [1152], replicated, may hold values from 0.5 to 1.5
- second_norm_bias: float32 [1152], replicated, may hold values from -3 to 3
- query_key_value_weight: bfloat16 [1152, 3, 1152], P('fsdp', None, 'heads'), may hold values from -0.1875 to 0.1875
- attention_output_weight: bfloat16 [1152, 1152], P('fsdp', 'heads'), may hold values from -3 to 3
- up_weight: bfloat16 [1152, 4304], P('fsdp', 'tensor'), may hold values from -0.1875 to 0.1875
- down_weight: bfloat16 [1152, 4304], P('fsdp', 'tensor'), may hold values from -0.09375 to 0.09375
- up_projection_bias: bfloat16 [4304], P('tensor'), may hold values from -3 to 3
- down_projection_bias: bfloat16 [1152], replicated, may hold values from -3 to 3
- query_key_value_adapter_first: bfloat16 [3, 8, 1152, 16], replicated, may hold values from -0.1875 to 0.1875
- query_key_value_adapter_second: bfloat16 [3, 8, 16, 1152], P(None, None, None, 'heads'), may hold values from -0.75 to 0.75
- projection_adapter_first: bfloat16 [8, 1152, 16], P(None, 'heads'), may hold values from -3 to 3
- projection_adapter_second: bfloat16 [8, 16, 1152], replicated, may hold values from -0.75 to 0.75
- up_adapter_first: bfloat16 [8, 1152, 16], replicated, may hold values from -0.1875 to 0.1875
- up_adapter_second: bfloat16 [8, 16, 4304], P(None, None, 'tensor'), may hold values from -0.75 to 0.75
- down_adapter_first: bfloat16 [8, 16, 4304], P(None, None, 'tensor'), may hold values from -0.09375 to 0.09375
- down_adapter_second: bfloat16 [8, 16, 1152], replicated, may hold values from -0.75 to 0.75
Outputs:
- layer_output: float32 [32, 729, 1152], P(('fsdp', 'heads', 'tensor'))
- grad_input: float32 [32, 729, 1152], P(('fsdp', 'heads', 'tensor'))
- grad_qkv_in: float32 [3, 8, 1152, 16], replicated
- grad_qkv_out: float32 [3, 8, 16, 1152], P(None, None, None, 'heads')
- grad_proj_in: float32 [8, 1152, 16], P(None, 'heads')
- grad_proj_out: float32 [8, 16, 1152], replicated
- grad_up_in: float32 [8, 1152, 16], replicated
- grad_up_out: float32 [8, 16, 4304], P(None, None, 'tensor')
- grad_down_in: float32 [8, 16, 4304], P(None, None, 'tensor')
- grad_down_out: float32 [8, 16, 1152], replicated
All inputs are finite; a program needn't handle non-finite values.
Results may differ from a plain program's by a relative error of at most 0.02.
Values may be sent and summed in bfloat16 or wider, within the bound.
A program may use at most 256 MiB of HBM per device.

v0:
```python
import jax
import jax.numpy as jnp
from jax import lax
from jax.sharding import PartitionSpec as P

HEAD_DIM = 72
highest_precision = lax.Precision.HIGHEST
norm_eps = 1e-06


def normalize(values, gain, bias):
    mean = jnp.mean(values, axis=-1, keepdims=True)
    centred = values - mean
    inverse = lax.rsqrt(jnp.mean(centred * centred, axis=-1, keepdims=True) + norm_eps)
    unit = centred * inverse
    return (unit * gain + bias, unit, inverse)


def normalize_back(grad_norm, unit, inverse, gain):
    scaled = grad_norm * gain
    return inverse * (
        scaled
        - jnp.mean(scaled, axis=-1, keepdims=True)
        - unit * jnp.mean(scaled * unit, axis=-1, keepdims=True)
    )


def gelu_tanh(values):
    return jax.nn.gelu(values, approximate=True)


def one_hot(ids, count):
    return (ids[:, None] == jnp.arange(count, dtype=jnp.int32)[None, :]).astype(jnp.float32)


def by_adapter(hot, per_image):
    return jnp.einsum("ia,ixy->axy", hot, per_image, precision=highest_precision)


def attend_forward(operands):
    query, keyed, valued = operands
    scores = jnp.einsum(
        "qhd,khd->hqk", query, keyed, preferred_element_type=jnp.float32
    ) * HEAD_DIM ** (-0.5)
    top = jnp.max(scores, axis=-1, keepdims=True)
    weights = jnp.exp(scores - top)
    total = jnp.sum(weights, axis=-1, keepdims=True)
    probs = (weights / total).astype(jnp.bfloat16)
    mixed_heads = jnp.einsum("hqk,khd->qhd", probs, valued, preferred_element_type=jnp.float32)
    return (mixed_heads.astype(jnp.bfloat16), (top + jnp.log(total))[..., 0])


def attend_back(operands):
    query, keyed, valued, grad_mixed, log_total = operands
    scale = HEAD_DIM ** (-0.5)
    scores = jnp.einsum("qhd,khd->hqk", query, keyed, preferred_element_type=jnp.float32) * scale
    probs = jnp.exp(scores - log_total[..., None])
    grad_probs = jnp.einsum("qhd,khd->hqk", grad_mixed, valued, preferred_element_type=jnp.float32)
    grad_values = jnp.einsum(
        "hqk,qhd->khd", probs.astype(jnp.bfloat16), grad_mixed, preferred_element_type=jnp.float32
    )
    inner = jnp.sum(probs * grad_probs, axis=-1, keepdims=True)
    grad_scores = (probs * (grad_probs - inner)).astype(jnp.bfloat16)
    grad_query = (
        jnp.einsum("hqk,khd->qhd", grad_scores, keyed, preferred_element_type=jnp.float32) * scale
    )
    grad_keys = (
        jnp.einsum("hqk,qhd->khd", grad_scores, query, preferred_element_type=jnp.float32) * scale
    )
    return (grad_query, grad_keys, grad_values)


def per_device(
    inputs,
    cotangent,
    image_adapter_index,
    first_norm_gain,
    first_norm_bias,
    second_norm_gain,
    second_norm_bias,
    query_key_value_weight,
    attention_output_weight,
    up_weight,
    down_weight,
    up_projection_bias,
    down_projection_bias,
    query_key_value_adapter_first,
    query_key_value_adapter_second,
    projection_adapter_first,
    projection_adapter_second,
    up_adapter_first,
    up_adapter_second,
    down_adapter_first,
    down_adapter_second,
):
    head_count = lax.axis_size("heads")
    unit_count = lax.axis_size("tensor")
    fsdp_index = lax.axis_index("fsdp")
    head_index = lax.axis_index("heads")
    unit_index = lax.axis_index("tensor")
    images, length, width = inputs.shape
    adapter_factors = query_key_value_adapter_first.shape[1]
    local = jnp.arange(images, dtype=jnp.int32)
    group = fsdp_index * head_count
    own_rows = ((group + head_index) * unit_count + unit_index) * images + local
    head_rows = (
        ((group + jnp.arange(head_count, dtype=jnp.int32))[:, None] * unit_count + unit_index)
        * images
        + local[None, :]
    ).reshape(-1)
    unit_rows = (
        ((group + head_index) * unit_count + jnp.arange(unit_count, dtype=jnp.int32))[:, None]
        * images
        + local[None, :]
    ).reshape(-1)
    owned_numbers = image_adapter_index[own_rows]
    head_numbers = image_adapter_index[head_rows]
    unit_numbers = image_adapter_index[unit_rows]
    query_key_value_whole, output_whole_weight, up_rows, down_rows = (
        lax.all_gather(query_key_value_weight, "fsdp", axis=0, tiled=True),
        lax.all_gather(attention_output_weight, "fsdp", axis=0, tiled=True),
        lax.all_gather(up_weight, "fsdp", axis=0, tiled=True),
        lax.all_gather(down_weight, "fsdp", axis=0, tiled=True),
    )
    norm1, unit1, inverse1 = normalize(inputs, first_norm_gain, first_norm_bias)
    ln1_all = lax.all_gather(norm1.astype(jnp.bfloat16), "heads", axis=0, tiled=True)
    (
        query_key_value_attention,
        output_attention_part,
        query_key_value_output_weight,
        projection_input_weight,
    ) = (
        query_key_value_whole,
        output_whole_weight,
        query_key_value_adapter_second,
        projection_adapter_first,
    )
    seen = ln1_all.shape[0]
    query_key_value_input_selected = query_key_value_adapter_first[:, head_numbers]
    qkv_out_sel = query_key_value_output_weight[:, head_numbers]
    query_key_value_middle = jnp.einsum(
        "obl,holm->hobm",
        ln1_all,
        query_key_value_input_selected,
        preferred_element_type=jnp.float32,
    )
    projected = jnp.einsum(
        "isd,djf->jisf", ln1_all, query_key_value_attention, preferred_element_type=jnp.float32
    )
    projected = projected + jnp.einsum(
        "klty,klye->klte",
        query_key_value_middle,
        qkv_out_sel.astype(jnp.float32),
        precision=highest_precision,
    )
    proj_low = projected.astype(jnp.bfloat16)
    local_width = proj_low.shape[-1]
    heads_local = local_width // HEAD_DIM
    shaped = proj_low.reshape(3, seen, length, heads_local, HEAD_DIM)
    mixed_heads, log_total = lax.map(attend_forward, (shaped[0], shaped[1], shaped[2]))
    mixed_heads = mixed_heads.reshape(seen, length, local_width)
    proj_in_sel = projection_input_weight[head_numbers]
    projection_output_selected = projection_adapter_second[head_numbers]
    projection_adapter_middle = jnp.einsum(
        "lby,lyg->lbg", mixed_heads, proj_in_sel, preferred_element_type=jnp.float32
    )
    attention_branch = jnp.einsum(
        "ise,de->isd", mixed_heads, output_attention_part, preferred_element_type=jnp.float32
    )
    attention_branch = attention_branch + jnp.einsum(
        "cmt,ctf->cmf",
        projection_adapter_middle,
        projection_output_selected.astype(jnp.float32),
        precision=highest_precision,
    )
    hidden = inputs + lax.psum_scatter(
        attention_branch.astype(jnp.bfloat16), "heads", scatter_dimension=0, tiled=True
    ).astype(jnp.float32)
    norm2, unit2, inverse2 = normalize(hidden, second_norm_gain, second_norm_bias)
    second_norm_reduced = norm2.astype(jnp.bfloat16)
    up_adapter_middle = jnp.einsum(
        "ego,eoh->egh",
        second_norm_reduced,
        up_adapter_first[owned_numbers],
        preferred_element_type=jnp.float32,
    ).astype(jnp.bfloat16)
    ln2_in, up_mid_in = (
        lax.all_gather(second_norm_reduced, "tensor", axis=0, tiled=True),
        lax.all_gather(up_adapter_middle, "tensor", axis=0, tiled=True),
    )
    up_cols, down_cols, bias_cols = (up_rows, down_rows, up_projection_bias)
    up_output_columns, down_input_columns = (up_adapter_second, down_adapter_first)
    up_input_selected = up_adapter_first[unit_numbers]
    up_out_sel = up_output_columns[unit_numbers]
    down_in_sel = down_input_columns[unit_numbers]
    down_output_selected = down_adapter_second[unit_numbers]
    residual_before = jnp.einsum(
        "isd,df->isf", ln2_in, up_cols, preferred_element_type=jnp.float32
    ) + bias_cols.astype(jnp.float32)
    residual_before = residual_before + jnp.einsum(
        "cbd,cdp->cbp",
        up_mid_in.astype(jnp.float32),
        up_out_sel.astype(jnp.float32),
        precision=highest_precision,
    )
    act_low = gelu_tanh(residual_before).astype(jnp.bfloat16)
    down_adapter_middle = jnp.einsum(
        "pco,pqo->pcq", act_low, down_in_sel, preferred_element_type=jnp.float32
    )
    mlp_part = jnp.einsum("isf,df->isd", act_low, down_cols, preferred_element_type=jnp.float32)
    mlp_part = mlp_part + jnp.einsum(
        "cmt,ctf->cmf",
        down_adapter_middle,
        down_output_selected.astype(jnp.float32),
        precision=highest_precision,
    )
    mlp_sum = lax.psum_scatter(
        mlp_part.astype(jnp.bfloat16), "tensor", scatter_dimension=0, tiled=True
    ).astype(jnp.float32)
    layer_output = hidden + mlp_sum + down_projection_bias.astype(jnp.float32)
    grad_mlp = cotangent.astype(jnp.bfloat16)
    grad_mlp_in = lax.all_gather(grad_mlp, "tensor", axis=0, tiled=True)
    grad_down_mid = jnp.einsum(
        "isd,ird->isr", grad_mlp_in, down_output_selected, preferred_element_type=jnp.float32
    )
    grad_act = jnp.einsum("isd,df->isf", grad_mlp_in, down_cols, preferred_element_type=jnp.float32)
    grad_act = grad_act + jnp.einsum(
        "cbd,cdp->cbp", grad_down_mid, down_in_sel.astype(jnp.float32), precision=highest_precision
    )
    ignored, gelu_pull = jax.vjp(gelu_tanh, residual_before)
    grad_before = gelu_pull(grad_act)[0].astype(jnp.bfloat16)
    grad_up_mid = jnp.einsum(
        "pco,pqo->pcq", grad_before, up_out_sel, preferred_element_type=jnp.float32
    )
    grad_ln2 = jnp.einsum("isf,df->isd", grad_before, up_cols, preferred_element_type=jnp.float32)
    grad_ln2 = grad_ln2 + jnp.einsum(
        "isr,idr->isd",
        grad_up_mid,
        up_input_selected.astype(jnp.float32),
        precision=highest_precision,
    )
    grad_ln2 = lax.psum_scatter(
        grad_ln2.astype(jnp.bfloat16), "tensor", scatter_dimension=0, tiled=True
    ).astype(jnp.float32)
    grad_hidden = cotangent + normalize_back(grad_ln2, unit2, inverse2, second_norm_gain)
    mlp_hot = one_hot(unit_numbers, adapter_factors)
    grad_up_in_part = by_adapter(
        mlp_hot, jnp.einsum("isd,isr->idr", ln2_in, grad_up_mid, precision=highest_precision)
    )
    grad_up_out_part = by_adapter(
        mlp_hot,
        jnp.einsum("isr,isf->irf", up_mid_in, grad_before, preferred_element_type=jnp.float32),
    )
    grad_down_in_part = by_adapter(
        mlp_hot, jnp.einsum("isr,isf->irf", grad_down_mid, act_low, precision=highest_precision)
    )
    grad_down_out_part = by_adapter(
        mlp_hot,
        jnp.einsum("isr,isd->ird", down_adapter_middle, grad_mlp_in, precision=highest_precision),
    )
    grad_branch = lax.all_gather(grad_hidden.astype(jnp.bfloat16), "heads", axis=0, tiled=True)
    grad_proj_mid = jnp.einsum(
        "isd,ird->isr", grad_branch, projection_output_selected, preferred_element_type=jnp.float32
    )
    grad_mixed = jnp.einsum(
        "isd,de->ise", grad_branch, output_attention_part, preferred_element_type=jnp.float32
    )
    grad_mixed = grad_mixed + jnp.einsum(
        "isr,ier->ise", grad_proj_mid, proj_in_sel.astype(jnp.float32), precision=highest_precision
    )
    grad_mixed = grad_mixed.astype(jnp.bfloat16).reshape(seen, length, heads_local, HEAD_DIM)
    grad_query, grad_keys, grad_values = lax.map(
        attend_back, (shaped[0], shaped[1], shaped[2], grad_mixed, log_total)
    )
    grad_proj = (
        jnp.stack([grad_query, grad_keys, grad_values])
        .reshape(3, seen, length, local_width)
        .astype(jnp.bfloat16)
    )
    grad_qkv_mid = jnp.einsum(
        "jisf,jirf->jisr", grad_proj, qkv_out_sel, preferred_element_type=jnp.float32
    )
    grad_ln1 = jnp.einsum(
        "jisf,djf->isd", grad_proj, query_key_value_attention, preferred_element_type=jnp.float32
    )
    grad_ln1 = grad_ln1 + jnp.einsum(
        "jisr,jidr->isd",
        grad_qkv_mid,
        query_key_value_input_selected.astype(jnp.float32),
        precision=highest_precision,
    )
    grad_ln1 = lax.psum_scatter(
        grad_ln1.astype(jnp.bfloat16), "heads", scatter_dimension=0, tiled=True
    ).astype(jnp.float32)
    grad_input = grad_hidden + normalize_back(grad_ln1, unit1, inverse1, first_norm_gain)
    attn_hot = one_hot(head_numbers, adapter_factors)
    qkv_in_image = jnp.einsum("isd,jisr->jidr", ln1_all, grad_qkv_mid, precision=highest_precision)
    grad_qkv_in_part = jnp.einsum(
        "ia,jidr->jadr", attn_hot, qkv_in_image, precision=highest_precision
    )
    qkv_out_image = jnp.einsum(
        "jisr,jisf->jirf", query_key_value_middle, grad_proj, precision=highest_precision
    )
    grad_qkv_out_part = jnp.einsum(
        "ia,jirf->jarf", attn_hot, qkv_out_image, precision=highest_precision
    )
    grad_proj_in_part = by_adapter(
        attn_hot,
        jnp.einsum("ise,isr->ier", mixed_heads, grad_proj_mid, precision=highest_precision),
    )
    grad_proj_out_part = by_adapter(
        attn_hot,
        jnp.einsum(
            "isr,isd->ird", projection_adapter_middle, grad_branch, precision=highest_precision
        ),
    )
    grad_qkv_in, grad_proj_out, grad_up_in, grad_down_out = lax.psum(
        (grad_qkv_in_part, grad_proj_out_part, grad_up_in_part, grad_down_out_part),
        ("fsdp", "heads", "tensor"),
    )
    grad_qkv_out, grad_proj_in = lax.psum(
        (grad_qkv_out_part, grad_proj_in_part), ("fsdp", "tensor")
    )
    grad_up_out, grad_down_in = (
        lax.psum(grad_up_out_part.astype(jnp.bfloat16), ("fsdp", "heads")).astype(jnp.float32),
        lax.psum(grad_down_in_part.astype(jnp.bfloat16), ("fsdp", "heads")).astype(jnp.float32),
    )
    return (
        layer_output,
        grad_input,
        grad_qkv_in,
        grad_qkv_out,
        grad_proj_in,
        grad_proj_out,
        grad_up_in,
        grad_up_out,
        grad_down_in,
        grad_down_out,
    )


def solution(mesh):
    in_specs = (
        P(("fsdp", "heads", "tensor"), None, None),
        P(("fsdp", "heads", "tensor"), None, None),
        P(),
        P(),
        P(),
        P(),
        P(),
        P("fsdp", None, "heads"),
        P("fsdp", "heads"),
        P("fsdp", "tensor"),
        P("fsdp", "tensor"),
        P("tensor"),
        P(),
        P(),
        P(None, None, None, "heads"),
        P(None, "heads", None),
        P(),
        P(),
        P(None, None, "tensor"),
        P(None, None, "tensor"),
        P(),
    )
    out_specs = (
        P(("fsdp", "heads", "tensor"), None, None),
        P(("fsdp", "heads", "tensor"), None, None),
        P(),
        P(None, None, None, "heads"),
        P(None, "heads", None),
        P(),
        P(),
        P(None, None, "tensor"),
        P(None, None, "tensor"),
        P(),
    )
    return jax.shard_map(
        per_device, mesh=mesh, in_specs=in_specs, out_specs=out_specs, check_vma=False
    )
```

profile of v0, /device:TPU:0, one launch (start us, length us, event | category | flops | bytes accessed | tf_op | source)
XLA Modules:
  0.0 1267.5 jit_solution(7760785568148674721)
XLA Ops:
  25.9 7.4 all-gather.11.cloned.1.call-done
  36.3 54.6 %all-gather.13.cloned.1.call-done = bf16[1152,3,576]{2,0,1:T(8,128)(2,1)} async-done(((bf16[288,3,576]{2,0,1:T(8,128)(2,1)}), bf16[1152,3,576]{2,0,1:T(8,128)(2,1)}) %all-gather.13.cloned.1.call-update) | async-done | bytes 3981328 | tf_op jit(solution)/shard_map/all_gather | solution.py:120
  90.9 10.7 fusion.59
  101.6 5.3 fusion.51
  109.1 57.2 %while.28 = (s32[]{:T(128)}, bf16[2,729,8,72]{1,3,2,0:T(8,128)(2,1)}, f32[2,8,729]{2,1,0:T(8,128)S(1)}, bf16[2,729,8,72]{1,3,2,0:T(8,128)(2,1)}, bf16[2,729,8,72...) while((s32[]{:T(128)}, bf16[2,729,8,72]{1,3,2,0:T(8,128)(2,1)}, ...), condition=%wide.region_5.6_spmd, body=%wide.region_2.5_spmd.sunk | while | flops 1263117824 | bytes 55831608 | solution.py:160
  109.1 9.9 multiply_reduce_fusion.8
  119.0 9.2 fusion.206
  128.2 9.3 fusion.207
  137.5 9.9 multiply_reduce_fusion.8
  147.4 9.2 fusion.206
  156.6 9.3 fusion.207
  168.9 5.0 fusion.84
  183.0 6.8 reduce-scatter.5.cloned.1.call-done
  202.4 102.8 %all-gather.23.cloned.1.call-done = bf16[4,729,1152]{2,1,0:T(8,128)(2,1)} async-done(((bf16[1,729,1152]{2,1,0:T(8,128)(2,1)}), bf16[4,729,1152]{2,1,0:T(8,128)(2,1)}) %all-gather.23.cloned.1.call-update) | async-done | bytes 6718480 | tf_op jit(solution)/shard_map/all_gather | solution.py:222
  310.0 34.9 %all-gather.21.cloned.1.call-done = bf16[1152,1076]{1,0:T(8,128)(2,1)} async-done(((bf16[288,1076]{1,0:T(8,128)(2,1)}), bf16[1152,1076]{1,0:T(8,128)(2,1)}) %all-gather.21.cloned.1.call-update) | async-done | bytes 2479120 | tf_op jit(solution)/shard_map/all_gather | solution.py:123
  344.9 14.5 %fusion.69 = f32[4,729,1076]{1,2,0:T(8,128)} fusion(bf16[4,729,1152]{2,1,0:T(8,128)(2,1)} %all-gather.23.cloned.1.call-done, bf16[1152,1076]{1,0:T(8,128)(2,1)} %all-gather.21.cloned.1.call-done), kind=kOutput, calls=%fused_computation.114 | convolution fusion | flops 7229067264 | bytes 21748032 | tf_op jit(solution)/shard_map/isd,df->isf/dot_general | solution.py:226
  359.9 13.3 %all-gather.1 = bf16[4,729,16]{1,2,0:T(8,128)(2,1)S(1)} all-gather(bf16[1,729,16]{1,2,0:T(8,128)(2,1)S(1)} %fusion.92), channel_id=2, replica_groups=mesh['fsdp'=4,'heads'=2,'tensor'=4] {'tensor'}, dimensions={0}, use_global_device_ids=true | all-gather | bytes 116640 | tf_op jit(solution)/shard_map/all_gather | solution.py:189
  373.2 13.1 %all-gather.19.cloned.1.call-done = bf16[1152,1076]{1,0:T(8,128)(2,1)} async-done(((bf16[288,1076]{1,0:T(8,128)(2,1)}), bf16[1152,1076]{1,0:T(8,128)(2,1)}) %all-gather.19.cloned.1.call-update) | async-done | bytes 2479120 | tf_op jit(solution)/shard_map/all_gather | solution.py:122
  386.4 124.8 %all-gather.17.cloned.1.call-done = bf16[4,729,1152]{2,1,0:T(8,128)(2,1)} async-done(((bf16[1,729,1152]{2,1,0:T(8,128)(2,1)}), bf16[4,729,1152]{2,1,0:T(8,128)(2,1)}) %all-gather.17.cloned.1.call-update) | async-done | bytes 6718480 | tf_op jit(solution)/shard_map/all_gather | solution.py:188
  511.2 12.4 fusion.75
  523.6 10.1 multiply_convert_fusion.1
  533.7 18.5 %fusion.50 = bf16[4,729,1076]{1,2,0:T(8,128)(2,1)S(1)} fusion(f32[4,729,1076]{1,2,0:T(8,128)} %get-tuple-element.204, f32[4,729,1076]{1,2,0:T(8,128)} %fusion.69, f32[4,16,729]{2,1,0:T(8,128)S(1)} %fusion.138, bf16[4,16,1076]{2,1,0:T(8,128)(2,1)S(1)} %gather_fusion.7), kind=kOutput, calls=%fused_computation.72 | convolution fusion | flops 668312192 | bytes 31700512 | tf_op jit(solution)/shard_map/cbd,cdp->cbp/dot_general | solution.py:227
  555.9 13.1 %fusion.73 = f32[4,729,1152]{2,1,0:T(8,128)} fusion(bf16[4,729,1076]{1,2,0:T(8,128)(2,1)S(1)} %fusion.50, bf16[1152,1076]{1,0:T(8,128)(2,1)S(1)} %copy-done.56), kind=kOutput, calls=%fused_computation.118 | convolution fusion | flops 7229067264 | bytes 22191264 | tf_op jit(solution)/shard_map/isf,df->isd/dot_general | solution.py:235
  569.0 10.8 add_convert_fusion
  583.9 13.5 %fusion.71 = f32[4,729,1152]{2,1,0:T(8,128)S(1)} fusion(bf16[4,729,1076]{1,2,0:T(8,128)(2,1)} %get-tuple-element.203, bf16[1152,1076]{1,0:T(8,128)(2,1)S(1)} %copy-done.55), kind=kOutput, calls=%fused_computation.116 | convolution fusion | flops 7229067264 | bytes 22191264 | tf_op jit(solution)/shard_map/isf,df->isd/dot_general | solution.py:210
  597.4 8.5 add_convert_fusion.1
  606.6 90.2 %reduce-scatter.9.cloned.1.call-done = bf16[1,729,1152]{2,1,0:T(8,128)(2,1)} async-done(((bf16[4,729,1152]{2,1,0:T(8,128)(2,1)}), bf16[1,729,1152]{2,1,0:T(8,128)(2,1)}) %reduce-scatter.9.cloned.1.call-update) | async-done | bytes 1679632 | tf_op jit(solution)/shard_map/reduce_scatter | solution.py:242
  700.4 118.0 %reduce-scatter.7.cloned.1.call-done = bf16[1,729,1152]{2,1,0:T(8,128)(2,1)} async-done(((bf16[4,729,1152]{2,1,0:T(8,128)(2,1)}), bf16[1,729,1152]{2,1,0:T(8,128)(2,1)}) %reduce-scatter.7.cloned.1.call-update) | async-done | bytes 1679632 | tf_op jit(solution)/shard_map/reduce_scatter | solution.py:217
  818.4 6.4 fusion.133
  824.9 7.5 fusion.145
  833.7 5.5 fusion.144
  840.5 5.1 fusion.146
  863.4 99.9 %while.29 = (s32[]{:T(128)}, bf16[2,729,8,72]{1,3,2,0:T(8,128)(2,1)}, bf16[2,729,8,72]{1,3,2,0:T(8,128)(2,1)}, bf16[2,729,8,72]{1,3,2,0:T(8,128)(2,1)}, bf16[2,7...) while((s32[]{:T(128)}, ...), condition=%wide.region_15.16_spmd, body=%wide.region_13.15_spmd.sunk | while | flops 3112952320 | bytes 200497152 | solution.py:272
  863.9 10.1 fusion.216
  873.9 8.1 bitcast_dynamic-update-slice_fusion.11
  882.1 12.7 %multiply_reduce_fusion.9 = (f32[8,729]{1,0:T(8,128)S(1)}, f32[8,729,729]{1,2,0:T(8,128)}) fusion(f32[8,729,729]{1,2,0:T(8,128)} %fusion.216, f32[8,729]{1,0:T(8,128)S(1)} %dynamic-slice_bitcast_fusion.2, bf16[2,729,8,72]{1,3,2,0:T(8,128)(2,1)S(1)} %copy-done.13, s32[]{:T(128)S(6)} %copy.187, bf16[2,729,8,72]{1,3,2,0:T(8,128)(2,1)S(1)} %copy-done.9), kind=kOutput, calls=%fused_computation.30.clone.1 | convolution fusion | flops 629220288 | bytes 35830624 | tf_op jit(solution)/shard_map/while/body/eval_jaxpr/qhd,khd->hqk/dot_general | solution.py:58
  894.8 13.2 %multiply_convert_fusion.3 = bf16[8,729,729]{1,2,0:T(8,128)(2,1)S(1)} fusion(f32[8,729,729]{1,2,0:T(8,128)} %get-tuple-element.305, f32[8,729,729]{1,2,0:T(8,128)} %fusion.216, f32[8,729]{1,0:T(8,128)S(1)} %get-tuple-element.306, f32[8,729]{1,0:T(8,128)S(1)} %dynamic-slice_bitcast_fusion.2), kind=kLoop, calls=%fused_computation.29.clone.1 | loop fusion | flops 21257640 | bytes 42561936 | tf_op jit(solution)/shard_map/while/body/eval_jaxpr/convert_element_type | solution.py:63
  913.8 10.0 fusion.216
  923.8 8.1 bitcast_dynamic-update-slice_fusion.11
  932.0 12.6 multiply_reduce_fusion.9
  944.5 13.1 %multiply_convert_fusion.3 = bf16[8,729,729]{1,2,0:T(8,128)(2,1)S(1)} fusion(f32[8,729,729]{1,2,0:T(8,128)} %get-tuple-element.305, f32[8,729,729]{1,2,0:T(8,128)} %fusion.216, f32[8,729]{1,0:T(8,128)S(1)} %get-tuple-element.306, f32[8,729]{1,0:T(8,128)S(1)} %dynamic-slice_bitcast_fusion.2), kind=kLoop, calls=%fused_computation.29.clone.1 | loop fusion | flops 21257640 | bytes 42561936 | tf_op jit(solution)/shard_map/while/body/eval_jaxpr/convert_element_type | solution.py:63
  963.4 6.3 fusion.53
  983.7 11.9 fusion.57
  1004.1 7.2 copy.104
  1011.3 76.5 %all-reduce.9.cloned.1.call-done = (f32[3,8,16,576]{3,1,2,0:T(8,128)}, f32[8,576,16]{1,0,2:T(8,128)}) async-done(((f32[3,8,16,576]{3,1,2,0:T(8,128)}, f32[8,576,16]{1,0,2:T(8,128)}), (f32[3,8,16,576]{3,1,2,0:T(8,128)}, f32[8,576,16]{1,0,2:T(8,128)})) %all-reduce.9.cloned.1.call-update) | async-done | bytes 1179664 | tf_op jit(solution)/shard_map/psum | solution.py:321
  1091.8 142.8 %all-reduce.7.cloned.1.call-done = (f32[3,8,1152,16]{2,1,3,0:T(8,128)}, f32[8,16,1152]{2,0,1:T(8,128)}, f32[8,1152,16]{1,0,2:T(8,128)}, f32[8,16,1152]{2,0,1:T(8,128)}) async-done(((f32[3,8,1152,16]{2,1,3,0:T(8,128)}, f32[8,16,1152]{2,0,1:T(8,128)}, f32[8,1152,16]{1,0,2:T(8,128)}, f32[8,16,1152]{2,0,1:T(8,128)}), (f32[3,8,1152,16]{2,1,3,0:T(8,128)}, f32[8,16,1152]{2,0,1:T(8,128)}, f32[8,1152,16]{1,0,2:T(8,128)}, ...) | async-done | bytes 3538960 | tf_op jit(solution)/shard_map/psum | solution.py:317
  1240.5 6.8 reduce-scatter.11.cloned.1.call-done
  1254.9 5.2 copy.105
  (272 shorter events, 134.1 us)
Async XLA Ops:
  8.0 17.2 %copy-start = (bf16[3,8,1152,16]{2,3,1,0:T(8,128)(2,1)S(1)}, bf16[3,8,1152,16]{2,3,1,0:T(8,128)(2,1)}, u32[]{:S(2)}) copy-start(bf16[3,8,1152,16]{2,3,1,0:T(8,128)(2,1)} %param.38) | copy-start | bytes 2654212
  8.0 8.0 copy-start.42
  8.0 8.0 copy-start.51
  8.0 25.2 %all-gather.11.cloned.1.call-start = ((), (), s32[]{:S(2)}) async-start(), calls=%async_computation.4 | async-start | bytes 5087232 | tf_op jit(solution)/shard_map/all_gather | solution.py:126
  17.9 73.0 %all-gather.13.cloned.1.call-start = ((), (), s32[]{:S(2)}) async-start(), calls=%async_computation.5 | async-start | bytes 5529600 | tf_op jit(solution)/shard_map/all_gather | solution.py:120
  18.6 150.3 %all-gather.15.cloned.1.call-start = ((), (), s32[]{:S(2)}) async-start(), calls=%async_computation.6 | async-start | bytes 1843200 | tf_op jit(solution)/shard_map/all_gather | solution.py:121
  19.4 170.4 %reduce-scatter.5.cloned.1.call-start = ((), (), s32[]{:S(2)}) async-start(), calls=%async_computation.7 | async-start | bytes 5087232 | tf_op jit(solution)/shard_map/reduce_scatter | solution.py:176
  25.2 76.4 %copy-start.32 = (bf16[2,3,16,576]{3,2,1,0:T(8,128)(2,1)}, bf16[2,3,16,576]{3,2,1,0:T(8,128)(2,1)S(1)}, u32[]{:S(2)}) copy-start(bf16[2,3,16,576]{3,2,1,0:T(8,128)(2,1)S(1)} %gather_fusion.2) | copy-start | bytes 331780
  25.8 75.8 %copy-start.11 = (bf16[2,3,1152,16]{2,3,1,0:T(8,128)(2,1)}, bf16[2,3,1152,16]{2,3,1,0:T(8,128)(2,1)S(1)}, u32[]{:S(2)}) copy-start(bf16[2,3,1152,16]{2,3,1,0:T(8,128)(2,1)S(1)} %gather_fusion.1) | copy-start | bytes 663556
  36.3 65.4 %copy-start.25 = (f32[3,2,729,16]{2,3,0,1:T(8,128)}, f32[3,2,729,16]{2,3,0,1:T(8,128)S(1)}, u32[]{:S(2)}) copy-start(f32[3,2,729,16]{2,3,0,1:T(8,128)S(1)} %fusion.86) | copy-start | bytes 839812
  109.1 57.2 %copy-start.21 = (bf16[2,576,16]{1,2,0:T(8,128)(2,1)S(1)}, bf16[2,576,16]{1,2,0:T(8,128)(2,1)}, u32[]{:S(2)}) copy-start(bf16[2,576,16]{1,2,0:T(8,128)(2,1)} %gather_fusion.3) | copy-start | bytes 110596
  166.3 7.6 copy-start.4
  166.3 7.6 copy-start.37
  178.4 126.8 %all-gather.23.cloned.1.call-start = ((), (), s32[]{:S(2)}) async-start(), calls=%async_computation.12 | async-start | bytes 8478720 | tf_op jit(solution)/shard_map/all_gather | solution.py:222
  181.8 163.1 %all-gather.21.cloned.1.call-start = ((), (), s32[]{:S(2)}) async-start(), calls=%async_computation.10 | async-start | bytes 3317760 | tf_op jit(solution)/shard_map/all_gather | solution.py:123
  182.4 204.0 %all-gather.19.cloned.1.call-start = ((), (), s32[]{:S(2)}) async-start(), calls=%async_computation.9 | async-start | bytes 3317760 | tf_op jit(solution)/shard_map/all_gather | solution.py:122
  182.9 328.3 %all-gather.17.cloned.1.call-start = ((), (), s32[]{:S(2)}) async-start(), calls=%async_computation.8 | async-start | bytes 8478720 | tf_op jit(solution)/shard_map/all_gather | solution.py:188
  196.7 500.0 %reduce-scatter.9.cloned.1.call-start = ((), (), s32[]{:S(2)}) async-start(), calls=%async_computation.13 | async-start | bytes 8478720 | tf_op jit(solution)/shard_map/reduce_scatter | solution.py:242
  310.0 49.4 %copy-start.14 = (bf16[1,729,1152]{2,1,0:T(8,128)(2,1)S(1)}, bf16[1,729,1152]{2,1,0:T(8,128)(2,1)}, u32[]{:S(2)}) copy-start(bf16[1,729,1152]{2,1,0:T(8,128)(2,1)} %add_convert_fusion.4) | copy-start | bytes 5038852
  373.2 150.3 %copy-start.34 = (bf16[4,729,16]{1,2,0:T(8,128)(2,1)}, bf16[4,729,16]{1,2,0:T(8,128)(2,1)S(1)}, u32[]{:S(2)}) copy-start(bf16[4,729,16]{1,2,0:T(8,128)(2,1)S(1)} %all-gather.1) | copy-start | bytes 279940
  579.8 238.6 %reduce-scatter.7.cloned.1.call-start = ((), (), s32[]{:S(2)}) async-start(), calls=%async_computation.11 | async-start | bytes 8478720 | tf_op jit(solution)/shard_map/reduce_scatter | solution.py:217
  605.9 245.4 %all-gather.25.cloned.1.call-start = ((), (), s32[]{:S(2)}) async-start(), calls=%async_computation.14 | async-start | bytes 5087232 | tf_op jit(solution)/shard_map/all_gather | solution.py:261
  696.8 121.6 %copy-start.18 = (bf16[1,729,1152]{2,1,0:T(8,128)(2,1)S(1)}, bf16[1,729,1152]{2,1,0:T(8,128)(2,1)}, u32[]{:S(2)}) copy-start(bf16[1,729,1152]{2,1,0:T(8,128)(2,1)} %reduce-scatter.9.cloned.1.call-done) | copy-start | bytes 5038852
  824.8 175.7 %all-reduce.11.cloned.1.call-start = ((), (), s32[]{:S(2)}) async-start(), calls=%async_computation.18 | async-start | bytes 1179648 | tf_op jit(solution)/shard_map/psum | solution.py:325
  824.9 8.8 copy-start.35
  833.7 13.3 %slice-start = ((s8[6782976]{0:T(1024)(128)(4,1)}), s8[2588672]{0:T(1024)(128)(4,1)S(1)}, s32[]{:S(2)}) async-start(s8[6782976]{0:T(1024)(128)(4,1)} %bitcast.261), calls=%async_computation.19 | async-start | bytes 5177344
  851.2 236.6 %all-reduce.9.cloned.1.call-start = ((), (), s32[]{:S(2)}) async-start(), calls=%async_computation.17 | async-start | bytes 2621440 | tf_op jit(solution)/shard_map/psum | solution.py:321
  863.4 99.9 %copy-start.26 = (f32[3,2,729,16]{2,3,0,1:T(8,128)S(1)}, f32[3,2,729,16]{2,3,0,1:T(8,128)}, u32[]{:S(2)}) copy-start(f32[3,2,729,16]{2,3,0,1:T(8,128)} %copy-done.25) | copy-start | bytes 839812
  863.8 10.1 copy-start.9
  863.9 10.1 copy-start.57
  873.9 8.1 copy-start.13
  882.1 12.7 %copy-start.58 = (bf16[2,729,8,72]{1,3,2,0:T(8,128)(2,1)}, bf16[2,729,8,72]{1,3,2,0:T(8,128)(2,1)S(1)}, u32[]{:S(2)}) copy-start(bf16[2,729,8,72]{1,3,2,0:T(8,128)(2,1)S(1)} %bitcast_dynamic-update-slice_fusion.11) | copy-start | bytes 5038852 | tf_op jit(solution)/shard_map/while
  894.8 13.3 %copy-start.6 = (bf16[2,729,8,72]{1,3,2,0:T(8,128)(2,1)S(1)}, bf16[2,729,8,72]{1,3,2,0:T(8,128)(2,1)}, u32[]{:S(2)}) copy-start(bf16[2,729,8,72]{1,3,2,0:T(8,128)(2,1)} %get-tuple-element.353) | copy-start | bytes 5038852 | tf_op jit(solution)/shard_map/while
  894.8 13.3 %copy-start.60 = (bf16[2,729,8,72]{1,3,2,0:T(8,128)(2,1)S(1)}, bf16[2,729,8,72]{1,3,2,0:T(8,128)(2,1)}, u32[]{:S(2)}) copy-start(bf16[2,729,8,72]{1,3,2,0:T(8,128)(2,1)} %get-tuple-element.340) | copy-start | bytes 5038852 | tf_op jit(solution)/shard_map/while
  913.8 10.1 copy-start.9
  913.8 10.1 copy-start.57
  923.8 8.1 copy-start.13
  931.9 12.6 copy-start.58
  944.5 13.1 %copy-start.6 = (bf16[2,729,8,72]{1,3,2,0:T(8,128)(2,1)S(1)}, bf16[2,729,8,72]{1,3,2,0:T(8,128)(2,1)}, u32[]{:S(2)}) copy-start(bf16[2,729,8,72]{1,3,2,0:T(8,128)(2,1)} %get-tuple-element.353) | copy-start | bytes 5038852 | tf_op jit(solution)/shard_map/while
  944.5 13.1 %copy-start.60 = (bf16[2,729,8,72]{1,3,2,0:T(8,128)(2,1)S(1)}, bf16[2,729,8,72]{1,3,2,0:T(8,128)(2,1)}, u32[]{:S(2)}) copy-start(bf16[2,729,8,72]{1,3,2,0:T(8,128)(2,1)} %get-tuple-element.340) | copy-start | bytes 5038852 | tf_op jit(solution)/shard_map/while
  963.3 9.1 copy-start.24
  972.4 262.2 %all-reduce.7.cloned.1.call-start = ((), (), s32[]{:S(2)}) async-start(), calls=%async_computation.16 | async-start | bytes 7077888 | tf_op jit(solution)/shard_map/psum | solution.py:317
  983.7 12.0 copy-start.12
  983.7 263.7 %reduce-scatter.11.cloned.1.call-start = ((), (), s32[]{:S(2)}) async-start(), calls=%async_computation.15 | async-start | bytes 5087232 | tf_op jit(solution)/shard_map/reduce_scatter | solution.py:292
  1234.6 12.7 %copy-start.40 = (f32[729]{0:T(1024)S(1)}, f32[729]{0:T(1024)}, u32[]{:S(2)}) copy-start(f32[729]{0:T(1024)} %copy-done.39) | copy-start | bytes 8752
  1234.6 12.7 %copy-start.43 = (f32[1152]{0:T(1024)S(1)}, f32[1152]{0:T(1024)}, u32[]{:S(2)}) copy-start(f32[1152]{0:T(1024)} %param.28) | copy-start | bytes 13828
  1234.7 12.7 %copy-start.48 = (f32[729]{0:T(1024)S(1)}, f32[729]{0:T(1024)}, u32[]{:S(2)}) copy-start(f32[729]{0:T(1024)} %copy-done.47) | copy-start | bytes 8752
  1251.1 9.0 copy-start.1
  (44 other events, 164.4 us)
Sparse Core Ops, SparseCore 0:
  18.0 15.1 all-gather.10
  35.0 55.7 all-gather.12
  92.7 30.1 all-gather.14
  178.5 11.2 reduce-scatter.4
  824.9 12.9 all-gather.24
  851.3 55.7 all-reduce.10
  972.6 115.1 all-reduce.8
  1094.9 139.7 all-reduce.6
  1237.0 10.2 reduce-scatter.10
Sparse Core Ops, SparseCore 1:
  181.9 123.2 all-gather.22
  306.9 37.9 all-gather.20
  346.6 39.7 all-gather.18
  387.9 123.2 all-gather.16
  579.9 116.8 reduce-scatter.8
  699.2 119.1 reduce-scatter.6
where the time goes:
time: 1270 us
  waiting for transfers between devices  781 us (61%)
  matrix products  326 us (26%)
  other arithmetic  77 us (6%)
  local copies, waits for them, and re-layouts  49.9 us (4%)
  between operations  18.4 us (1%)
  blocking collectives  13.3 us (1%)
    psum x1, waiting for transfers between devices, per_device(): lax.psum((grad_qkv_in_part, grad_proj_out_part, grad_up_in_part, grad_dow...  143 us
    all_gather x1, waiting for transfers between devices, per_device(): lax.all_gather(second_norm_reduced, 'tensor', axis=0, tiled=True)  125 us
    reduce_scatter x1, waiting for transfers between devices, per_device(): lax.psum_scatter(mlp_part.astype(jnp.bfloat16), 'tensor', scatter_dimensi...  118 us
    all_gather x1, waiting for transfers between devices, per_device(): grad_mlp_in = lax.all_gather(grad_mlp, 'tensor', axis=0, tiled=True)  103 us
    reduce_scatter x1, waiting for transfers between devices, per_device(): lax.psum_scatter(grad_ln2.astype(jnp.bfloat16), 'tensor', scatter_dimensi...  90.2 us
    psum x1, waiting for transfers between devices, per_device(): lax.psum((grad_qkv_out_part, grad_proj_in_part), ('fsdp', 'tensor'))  76.5 us
    all_gather x1, waiting for transfers between devices, per_device(): lax.all_gather(query_key_value_weight, 'fsdp', axis=0, tiled=True)  54.6 us
    unnamed x129, local copies, waits for them, and re-layouts  35.5 us
  transfers between devices with their start and end apart: 15, of which 12 were waited for; matrix products, arithmetic and copies ran while one was open for 27% of the time, Pallas kernels for 0%

commit v1 on v0

--- a/solution.py
+++ b/solution.py
@@ -6,6 +6,27 @@
 HEAD_DIM = 72
 highest_precision = lax.Precision.HIGHEST
 norm_eps = 1e-06
+
+
+def collect(x, axis, dim):
+    count, index, rows = (lax.axis_size(axis), lax.axis_index(axis), x.shape[dim])
+    right = [(i, (i + 1) % count) for i in range(count)]
+    backward = [(i, (i - 1) % count) for i in range(count)]
+    result = jnp.zeros((*x.shape[:dim], count * rows, *x.shape[dim + 1 :]), x.dtype)
+    result = lax.dynamic_update_slice_in_dim(result, x, index * rows, axis=dim)
+    from_left = from_right = x
+    middle = count // 2
+    for step in range(1, middle + 1):
+        from_left = lax.ppermute(from_left, axis, right)
+        result = lax.dynamic_update_slice_in_dim(
+            result, from_left, (index - step) % count * rows, axis=dim
+        )
+        if step < count - middle:
+            from_right = lax.ppermute(from_right, axis, backward)
+            result = lax.dynamic_update_slice_in_dim(
+                result, from_right, (index + step) % count * rows, axis=dim
+            )
+    return result
 
 
 def normalize(values, gain, bias):
@@ -120,7 +141,7 @@
         lax.all_gather(query_key_value_weight, "fsdp", axis=0, tiled=True),
         lax.all_gather(attention_output_weight, "fsdp", axis=0, tiled=True),
         lax.all_gather(up_weight, "fsdp", axis=0, tiled=True),
-        lax.all_gather(down_weight, "fsdp", axis=0, tiled=True),
+        collect(down_weight, "fsdp", 0),
     )
     norm1, unit1, inverse1 = normalize(inputs, first_norm_gain, first_norm_bias)
     ln1_all = lax.all_gather(norm1.astype(jnp.bfloat16), "heads", axis=0, tiled=True)

time: 1270 us -> 1230 us (0.969)
  waiting for transfers between devices: 781 us -> 698 us
  local copies, waits for them, and re-layouts: 49.9 us -> 93.3 us
    all_gather x1, waiting for transfers between devices: 103 us -> 37.8 us  [per_device(): grad_mlp_in = lax.all_gather(grad_mlp, 'tensor', axis=0, tiled=True)]
    dynamic_update_slice x0 -> x4, local copies, waits for them, and re-layouts: none -> 37.4 us  [the longest x2 18.9 us: collect(): lax.dynamic_update_slice_in_dim(result, from_left, (index - step) % count...]
    all_gather x1 -> x0, waiting for transfers between devices: 34.9 us -> none  [per_device(): lax.all_gather(down_weight, 'fsdp', axis=0, tiled=True)]
    ppermute x0 -> x3, waiting for transfers between devices: none -> 15.7 us  [the longest x2 15.7 us: collect(): from_left = lax.ppermute(from_left, axis, right)]
    unnamed x129 -> x134, local copies, waits for them, and re-layouts: 35.5 us -> 34 us
  transfers between devices with their start and end apart: 15 -> 17, of which waited for: 12 -> 12; matrix products, arithmetic and copies ran while one was open for 27% -> 31% of each run, Pallas kernels for 0% -> 0%
where the time goes in v1:
time: 1230 us
  waiting for transfers between devices  698 us (57%)
  matrix products  321 us (26%)
  local copies, waits for them, and re-layouts  93.3 us (8%)
  other arithmetic  77 us (6%)
  between operations  18.7 us (2%)
  blocking collectives  13.4 us (1%)
    psum x1, waiting for transfers between devices, per_device(): lax.psum((grad_qkv_in_part, grad_proj_out_part, grad_up_in_part, grad_dow...  143 us
    all_gather x1, waiting for transfers between devices, per_device(): lax.all_gather(second_norm_reduced, 'tensor', axis=0, tiled=True)  125 us
    reduce_scatter x1, waiting for transfers between devices, per_device(): lax.psum_scatter(mlp_part.astype(jnp.bfloat16), 'tensor', scatter_dimensi...  118 us
    reduce_scatter x1, waiting for transfers between devices, per_device(): lax.psum_scatter(grad_ln2.astype(jnp.bfloat16), 'tensor', scatter_dimensi...  92 us
    psum x1, waiting for transfers between devices, per_device(): lax.psum((grad_qkv_out_part, grad_proj_in_part), ('fsdp', 'tensor'))  76.4 us
    all_gather x1, waiting for transfers between devices, per_device(): lax.all_gather(query_key_value_weight, 'fsdp', axis=0, tiled=True)  54.6 us
    all_gather x1, waiting for transfers between devices, per_device(): grad_mlp_in = lax.all_gather(grad_mlp, 'tensor', axis=0, tiled=True)  37.8 us
    unnamed x134, local copies, waits for them, and re-layouts  34 us
  transfers between devices with their start and end apart: 17, of which 12 were waited for; matrix products, arithmetic and copies ran while one was open for 31% of the time, Pallas kernels for 0%

profile of v1, /device:TPU:0, one launch (start us, length us, event | category | flops | bytes accessed | tf_op | source)
XLA Modules:
  0.0 1227.3 jit_solution(2007373508250236518)
XLA Ops:
  25.8 7.4 all-gather.10.cloned.1.call-done
  36.3 54.6 %all-gather.12.cloned.1.call-done = bf16[1152,3,576]{2,0,1:T(8,128)(2,1)} async-done(((bf16[288,3,576]{2,0,1:T(8,128)(2,1)}), bf16[1152,3,576]{2,0,1:T(8,128)(2,1)}) %all-gather.12.cloned.1.call-update) | async-done | bytes 3981328 | tf_op jit(solution)/shard_map/all_gather | solution.py:141
  90.9 10.7 fusion.59
  109.1 57.3 %while.28 = (s32[]{:T(128)}, bf16[2,729,8,72]{1,3,2,0:T(8,128)(2,1)}, f32[2,8,729]{2,1,0:T(8,128)S(1)}, bf16[2,729,8,72]{1,3,2,0:T(8,128)(2,1)}, bf16[2,729,8,72...) while((s32[]{:T(128)}, bf16[2,729,8,72]{1,3,2,0:T(8,128)(2,1)}, ...), condition=%wide.region_5.6_spmd, body=%wide.region_2.5_spmd.sunk | while | flops 1263117824 | bytes 55831608 | solution.py:181
  109.1 9.9 multiply_reduce_fusion.8
  119.1 9.2 fusion.206
  128.3 9.3 fusion.207
  137.6 9.9 multiply_reduce_fusion.8
  147.5 9.2 fusion.206
  156.7 9.3 fusion.207
  182.5 7.3 reduce-scatter.5.cloned.1.call-done
  199.9 15.7 %collective-permute-done = bf16[288,1076]{1,0:T(8,128)(2,1)S(1)} collective-permute-done((bf16[288,1076]{1,0:T(8,128)(2,1)S(1)}, bf16[288,1076]{1,0:T(8,128)(2,1)S(1)}, u32[]{:S(2)}, u32[]{:S(2)}) %collective-permute-start) | collective-permute-done | bytes 619808 | tf_op jit(solution)/shard_map/ppermute | solution.py:20
  226.7 8.7 dynamic_update_slice.30
  235.8 9.1 dynamic_update_slice.31
  246.4 9.8 dynamic_update_slice.32
  257.7 9.7 dynamic_update_slice.33
  267.4 37.8 %all-gather.20.cloned.1.call-done = bf16[4,729,1152]{2,1,0:T(8,128)(2,1)} async-done(((bf16[1,729,1152]{2,1,0:T(8,128)(2,1)}), bf16[4,729,1152]{2,1,0:T(8,128)(2,1)}) %all-gather.20.cloned.1.call-update) | async-done | bytes 6718480 | tf_op jit(solution)/shard_map/all_gather | solution.py:243
  310.1 8.4 fusion.138
  319.0 13.4 %all-gather.1 = bf16[4,729,16]{1,2,0:T(8,128)(2,1)S(1)} all-gather(bf16[1,729,16]{1,2,0:T(8,128)(2,1)S(1)} %fusion.90), channel_id=2, replica_groups=mesh['fsdp'=4,'heads'=2,'tensor'=4] {'tensor'}, dimensions={0}, use_global_device_ids=true | all-gather | bytes 116640 | tf_op jit(solution)/shard_map/all_gather | solution.py:210
  332.4 12.6 %all-gather.18.cloned.1.call-done = bf16[1152,1076]{1,0:T(8,128)(2,1)} async-done(((bf16[288,1076]{1,0:T(8,128)(2,1)}), bf16[1152,1076]{1,0:T(8,128)(2,1)}) %all-gather.18.cloned.1.call-update) | async-done | bytes 2479120 | tf_op jit(solution)/shard_map/all_gather | solution.py:143
  344.9 124.7 %all-gather.16.cloned.1.call-done = bf16[4,729,1152]{2,1,0:T(8,128)(2,1)} async-done(((bf16[1,729,1152]{2,1,0:T(8,128)(2,1)}), bf16[4,729,1152]{2,1,0:T(8,128)(2,1)}) %all-gather.16.cloned.1.call-update) | async-done | bytes 6718480 | tf_op jit(solution)/shard_map/all_gather | solution.py:209
  469.6 12.4 %fusion.71 = f32[4,729,1076]{1,2,0:T(8,128)S(1)} fusion(bf16[4,729,1152]{2,1,0:T(8,128)(2,1)} %all-gather.16.cloned.1.call-done, bf16[1152,1076]{1,0:T(8,128)(2,1)} %all-gather.18.cloned.1.call-done), kind=kOutput, calls=%fused_computation.117 | convolution fusion | flops 7229067264 | bytes 21748032 | tf_op jit(solution)/shard_map/isd,df->isf/dot_general | solution.py:218
  482.0 10.0 multiply_convert_fusion.1
  492.1 22.6 %fusion.50 = bf16[4,729,1076]{1,2,0:T(8,128)(2,1)} fusion(f32[4,729,1076]{1,2,0:T(8,128)} %get-tuple-element.204, f32[4,729,1076]{1,2,0:T(8,128)} %fusion.138, bf16[4,729,1152]{2,1,0:T(8,128)(2,1)} %all-gather.20.cloned.1.call-done, bf16[1152,1076]{0,1:T(8,128)(2,1)S(1)} %copy-done.23), kind=kOutput, calls=%fused_computation.72 | convolution fusion | flops 7294955520 | bytes 40573728 | tf_op jit(solution)/shard_map/isd,df->isf/dot_general | solution.py:247
  519.4 11.8 fusion.69
  531.2 8.3 add_convert_fusion
  543.5 5.6 fusion.136
  549.1 14.8 %add_convert_fusion.1 = bf16[4,729,1152]{2,1,0:T(8,128)(2,1)} fusion(f32[4,729,1152]{2,1,0:T(8,128)S(1)} %fusion.136, bf16[4,729,1076]{1,2,0:T(8,128)(2,1)} %get-tuple-element.203, bf16[1152,1076]{0,1:T(8,128)(2,1)S(1)} %copy-done.23), kind=kOutput, calls=%fused_computation.65 | convolution fusion | flops 7235785728 | bytes 28909728 | tf_op jit(solution)/shard_map/isf,df->isd/dot_general | solution.py:231
  564.5 92.0 %reduce-scatter.9.cloned.1.call-done = bf16[1,729,1152]{2,1,0:T(8,128)(2,1)} async-done(((bf16[4,729,1152]{2,1,0:T(8,128)(2,1)}), bf16[1,729,1152]{2,1,0:T(8,128)(2,1)}) %reduce-scatter.9.cloned.1.call-update) | async-done | bytes 1679632 | tf_op jit(solution)/shard_map/reduce_scatter | solution.py:263
  660.1 118.0 %reduce-scatter.7.cloned.1.call-done = bf16[1,729,1152]{2,1,0:T(8,128)(2,1)} async-done(((bf16[4,729,1152]{2,1,0:T(8,128)(2,1)}), bf16[1,729,1152]{2,1,0:T(8,128)(2,1)}) %reduce-scatter.7.cloned.1.call-update) | async-done | bytes 1679632 | tf_op jit(solution)/shard_map/reduce_scatter | solution.py:238
  778.1 6.3 fusion.131
  784.6 7.5 fusion.145
  793.4 5.5 fusion.144
  823.1 100.0 %while.29 = (s32[]{:T(128)}, bf16[2,729,8,72]{1,3,2,0:T(8,128)(2,1)}, bf16[2,729,8,72]{1,3,2,0:T(8,128)(2,1)}, bf16[2,729,8,72]{1,3,2,0:T(8,128)(2,1)}, bf16[2,7...) while((s32[]{:T(128)}, ...), condition=%wide.region_15.16_spmd, body=%wide.region_13.15_spmd.sunk | while | flops 3112952320 | bytes 200497152 | solution.py:293
  823.6 10.1 fusion.216
  833.7 8.1 bitcast_dynamic-update-slice_fusion.11
  841.9 12.6 %multiply_reduce_fusion.9 = (f32[8,729]{1,0:T(8,128)S(1)}, f32[8,729,729]{1,2,0:T(8,128)}) fusion(f32[8,729,729]{1,2,0:T(8,128)} %fusion.216, f32[8,729]{1,0:T(8,128)S(1)} %dynamic-slice_bitcast_fusion.2, bf16[2,729,8,72]{1,3,2,0:T(8,128)(2,1)S(1)} %copy-done.13, s32[]{:T(128)S(6)} %copy.203, bf16[2,729,8,72]{1,3,2,0:T(8,128)(2,1)S(1)} %copy-done.9), kind=kOutput, calls=%fused_computation.30.clone.1 | convolution fusion | flops 629220288 | bytes 35830624 | tf_op jit(solution)/shard_map/while/body/eval_jaxpr/qhd,khd->hqk/dot_general | solution.py:79
  854.5 13.2 %multiply_convert_fusion.3 = bf16[8,729,729]{1,2,0:T(8,128)(2,1)S(1)} fusion(f32[8,729,729]{1,2,0:T(8,128)} %get-tuple-element.305, f32[8,729,729]{1,2,0:T(8,128)} %fusion.216, f32[8,729]{1,0:T(8,128)S(1)} %get-tuple-element.306, f32[8,729]{1,0:T(8,128)S(1)} %dynamic-slice_bitcast_fusion.2), kind=kLoop, calls=%fused_computation.29.clone.1 | loop fusion | flops 21257640 | bytes 42561936 | tf_op jit(solution)/shard_map/while/body/eval_jaxpr/convert_element_type | solution.py:84
  873.5 10.1 fusion.216
  883.6 8.1 bitcast_dynamic-update-slice_fusion.11
  891.7 12.5 %multiply_reduce_fusion.9 = (f32[8,729]{1,0:T(8,128)S(1)}, f32[8,729,729]{1,2,0:T(8,128)}) fusion(f32[8,729,729]{1,2,0:T(8,128)} %fusion.216, f32[8,729]{1,0:T(8,128)S(1)} %dynamic-slice_bitcast_fusion.2, bf16[2,729,8,72]{1,3,2,0:T(8,128)(2,1)S(1)} %copy-done.13, s32[]{:T(128)S(6)} %copy.203, bf16[2,729,8,72]{1,3,2,0:T(8,128)(2,1)S(1)} %copy-done.9), kind=kOutput, calls=%fused_computation.30.clone.1 | convolution fusion | flops 629220288 | bytes 35830624 | tf_op jit(solution)/shard_map/while/body/eval_jaxpr/qhd,khd->hqk/dot_general | solution.py:79
  904.2 13.2 %multiply_convert_fusion.3 = bf16[8,729,729]{1,2,0:T(8,128)(2,1)S(1)} fusion(f32[8,729,729]{1,2,0:T(8,128)} %get-tuple-element.305, f32[8,729,729]{1,2,0:T(8,128)} %fusion.216, f32[8,729]{1,0:T(8,128)S(1)} %get-tuple-element.306, f32[8,729]{1,0:T(8,128)S(1)} %dynamic-slice_bitcast_fusion.2), kind=kLoop, calls=%fused_computation.29.clone.1 | loop fusion | flops 21257640 | bytes 42561936 | tf_op jit(solution)/shard_map/while/body/eval_jaxpr/convert_element_type | solution.py:84
  923.1 6.3 fusion.53
  943.5 11.9 fusion.57
  963.9 7.2 copy.116
  971.1 76.4 %all-reduce.9.cloned.1.call-done = (f32[3,8,16,576]{3,1,2,0:T(8,128)}, f32[8,576,16]{1,0,2:T(8,128)}) async-done(((f32[3,8,16,576]{3,1,2,0:T(8,128)}, f32[8,576,16]{1,0,2:T(8,128)}), (f32[3,8,16,576]{3,1,2,0:T(8,128)}, f32[8,576,16]{1,0,2:T(8,128)})) %all-reduce.9.cloned.1.call-update) | async-done | bytes 1179664 | tf_op jit(solution)/shard_map/psum | solution.py:342
  1051.5 142.8 %all-reduce.7.cloned.1.call-done = (f32[3,8,1152,16]{2,1,3,0:T(8,128)}, f32[8,16,1152]{2,0,1:T(8,128)}, f32[8,1152,16]{1,0,2:T(8,128)}, f32[8,16,1152]{2,0,1:T(8,128)}) async-done(((f32[3,8,1152,16]{2,1,3,0:T(8,128)}, f32[8,16,1152]{2,0,1:T(8,128)}, f32[8,1152,16]{1,0,2:T(8,128)}, f32[8,16,1152]{2,0,1:T(8,128)}), (f32[3,8,1152,16]{2,1,3,0:T(8,128)}, f32[8,16,1152]{2,0,1:T(8,128)}, f32[8,1152,16]{1,0,2:T(8,128)}, ...) | async-done | bytes 3538960 | tf_op jit(solution)/shard_map/psum | solution.py:338
  1200.2 6.8 reduce-scatter.11.cloned.1.call-done
  (288 shorter events, 167.0 us)
Async XLA Ops:
  8.0 17.2 %copy-start = (bf16[3,8,1152,16]{2,3,1,0:T(8,128)(2,1)S(1)}, bf16[3,8,1152,16]{2,3,1,0:T(8,128)(2,1)}, u32[]{:S(2)}) copy-start(bf16[3,8,1152,16]{2,3,1,0:T(8,128)(2,1)} %param.38) | copy-start | bytes 2654212
  8.0 25.2 %all-gather.10.cloned.1.call-start = ((), (), s32[]{:S(2)}) async-start(), calls=%async_computation.4 | async-start | bytes 5087232 | tf_op jit(solution)/shard_map/all_gather | solution.py:147
  17.9 73.0 %all-gather.12.cloned.1.call-start = ((), (), s32[]{:S(2)}) async-start(), calls=%async_computation.5 | async-start | bytes 5529600 | tf_op jit(solution)/shard_map/all_gather | solution.py:141
  18.6 150.3 %all-gather.14.cloned.1.call-start = ((), (), s32[]{:S(2)}) async-start(), calls=%async_computation.6 | async-start | bytes 1843200 | tf_op jit(solution)/shard_map/all_gather | solution.py:142
  19.4 170.4 %reduce-scatter.5.cloned.1.call-start = ((), (), s32[]{:S(2)}) async-start(), calls=%async_computation.7 | async-start | bytes 5087232 | tf_op jit(solution)/shard_map/reduce_scatter | solution.py:197
  25.2 76.4 %copy-start.38 = (bf16[2,3,16,576]{3,2,1,0:T(8,128)(2,1)}, bf16[2,3,16,576]{3,2,1,0:T(8,128)(2,1)S(1)}, u32[]{:S(2)}) copy-start(bf16[2,3,16,576]{3,2,1,0:T(8,128)(2,1)S(1)} %gather_fusion.2) | copy-start | bytes 331780
  25.8 75.8 %copy-start.11 = (bf16[2,3,1152,16]{2,3,1,0:T(8,128)(2,1)}, bf16[2,3,1152,16]{2,3,1,0:T(8,128)(2,1)S(1)}, u32[]{:S(2)}) copy-start(bf16[2,3,1152,16]{2,3,1,0:T(8,128)(2,1)S(1)} %gather_fusion.1) | copy-start | bytes 663556
  36.3 65.4 %copy-start.28 = (f32[3,2,729,16]{2,3,0,1:T(8,128)}, f32[3,2,729,16]{2,3,0,1:T(8,128)S(1)}, u32[]{:S(2)}) copy-start(f32[3,2,729,16]{2,3,0,1:T(8,128)S(1)} %fusion.84) | copy-start | bytes 839812
  109.1 57.3 %copy-start.21 = (bf16[2,576,16]{1,2,0:T(8,128)(2,1)S(1)}, bf16[2,576,16]{1,2,0:T(8,128)(2,1)}, u32[]{:S(2)}) copy-start(bf16[2,576,16]{1,2,0:T(8,128)(2,1)} %gather_fusion.3) | copy-start | bytes 110596
  178.4 126.8 %all-gather.20.cloned.1.call-start = ((), (), s32[]{:S(2)}) async-start(), calls=%async_computation.11 | async-start | bytes 8478720 | tf_op jit(solution)/shard_map/all_gather | solution.py:243
  181.9 163.1 %all-gather.18.cloned.1.call-start = ((), (), s32[]{:S(2)}) async-start(), calls=%async_computation.9 | async-start | bytes 3317760 | tf_op jit(solution)/shard_map/all_gather | solution.py:143
  182.5 287.2 %all-gather.16.cloned.1.call-start = ((), (), s32[]{:S(2)}) async-start(), calls=%async_computation.8 | async-start | bytes 8478720 | tf_op jit(solution)/shard_map/all_gather | solution.py:209
  195.0 21.9 %copy-start.3 = (s32[32]{0:T(128)S(1)}, s32[32]{0:T(128)}, u32[]{:S(2)}) copy-start(s32[32]{0:T(128)} %param.27) | copy-start | bytes 388
  195.0 24.5 %copy-start.57 = (bf16[1076]{0:T(1024)(128)(2,1)S(1)}, bf16[1076]{0:T(1024)(128)(2,1)}, u32[]{:S(2)}) copy-start(bf16[1076]{0:T(1024)(128)(2,1)} %param.36) | copy-start | bytes 6460
  195.0 24.5 %copy-start.50 = (bf16[8,16,1152]{2,1,0:T(8,128)(2,1)S(1)}, bf16[8,16,1152]{2,1,0:T(8,128)(2,1)}, u32[]{:S(2)}) copy-start(bf16[8,16,1152]{2,1,0:T(8,128)(2,1)} %param.45) | copy-start | bytes 884740
  196.8 27.0 %copy-start.20 = (bf16[8,1152,16]{1,2,0:T(8,128)(2,1)S(1)}, bf16[8,1152,16]{1,2,0:T(8,128)(2,1)}, u32[]{:S(2)}) copy-start(bf16[8,1152,16]{1,2,0:T(8,128)(2,1)} %param.42) | copy-start | bytes 884740
  196.8 459.6 %reduce-scatter.9.cloned.1.call-start = ((), (), s32[]{:S(2)}) async-start(), calls=%async_computation.12 | async-start | bytes 8478720 | tf_op jit(solution)/shard_map/reduce_scatter | solution.py:263
  196.9 18.7 %collective-permute-start = (bf16[288,1076]{1,0:T(8,128)(2,1)S(1)}, bf16[288,1076]{1,0:T(8,128)(2,1)S(1)}, u32[]{:S(2)}, u32[]{:S(2)}) collective-permute-start(bf16[288,1076]{1,0:T(8,128)(2,1)S(1)} %copy-done.30), channel_id=1, source_target_pairs={{0,8},{8,16},{16,24},{24,0},{1,9},{9,17},{17,25},{25,1},{2,10},{10... | collective-permute-start | bytes 1859336 | tf_op jit(solution)/shard_map/ppermute | solution.py:20
  198.7 46.2 %collective-permute-start.1 = (bf16[288,1076]{1,0:T(8,128)(2,1)S(1)}, bf16[288,1076]{1,0:T(8,128)(2,1)}, u32[]{:S(2)}, u32[]{:S(2)}) collective-permute-start(bf16[288,1076]{1,0:T(8,128)(2,1)S(1)} %copy-done.30), channel_id=1, source_target_pairs={{0,24},{8,0},{16,8},{24,16},{1,25},{9,1},{17,9},{25,17},{2,26},{10... | collective-permute-start | bytes 1859336 | tf_op jit(solution)/shard_map/ppermute | solution.py:25
  215.6 40.6 %collective-permute-start.2 = (bf16[288,1076]{1,0:T(8,128)(2,1)S(1)}, bf16[288,1076]{1,0:T(8,128)(2,1)}, u32[]{:S(2)}, u32[]{:S(2)}) collective-permute-start(bf16[288,1076]{1,0:T(8,128)(2,1)S(1)} %collective-permute-done), channel_id=1, source_target_pairs={{0,8},{8,16},{16,24},{24,0},{1,9},{9,17},{17,25},{25,1},{2,10},{10... | collective-permute-start | bytes 1859336 | tf_op jit(solution)/shard_map/ppermute | solution.py:20
  220.0 85.2 %copy-start.24 = (bf16[4,16,1152]{2,1,0:T(8,128)(2,1)}, bf16[4,16,1152]{2,1,0:T(8,128)(2,1)S(1)}, u32[]{:S(2)}) copy-start(bf16[4,16,1152]{2,1,0:T(8,128)(2,1)S(1)} %gather_fusion.8) | copy-start | bytes 442372
  332.4 149.6 %copy-start.40 = (bf16[4,729,16]{1,2,0:T(8,128)(2,1)}, bf16[4,729,16]{1,2,0:T(8,128)(2,1)S(1)}, u32[]{:S(2)}) copy-start(bf16[4,729,16]{1,2,0:T(8,128)(2,1)S(1)} %all-gather.1) | copy-start | bytes 279940
  332.4 149.6 %copy-start.33 = (bf16[4,16,1076]{2,1,0:T(8,128)(2,1)S(1)}, bf16[4,16,1076]{2,1,0:T(8,128)(2,1)}, u32[]{:S(2)}) copy-start(bf16[4,16,1076]{2,1,0:T(8,128)(2,1)} %gather_fusion.6) | copy-start | bytes 413188
  482.0 10.1 copy-start.23
  539.5 238.6 %reduce-scatter.7.cloned.1.call-start = ((), (), s32[]{:S(2)}) async-start(), calls=%async_computation.10 | async-start | bytes 8478720 | tf_op jit(solution)/shard_map/reduce_scatter | solution.py:238
  563.9 247.1 %all-gather.22.cloned.1.call-start = ((), (), s32[]{:S(2)}) async-start(), calls=%async_computation.13 | async-start | bytes 5087232 | tf_op jit(solution)/shard_map/all_gather | solution.py:282
  656.5 121.6 %copy-start.18 = (bf16[1,729,1152]{2,1,0:T(8,128)(2,1)S(1)}, bf16[1,729,1152]{2,1,0:T(8,128)(2,1)}, u32[]{:S(2)}) copy-start(bf16[1,729,1152]{2,1,0:T(8,128)(2,1)} %reduce-scatter.9.cloned.1.call-done) | copy-start | bytes 5038852
  784.5 175.8 %all-reduce.11.cloned.1.call-start = ((), (), s32[]{:S(2)}) async-start(), calls=%async_computation.17 | async-start | bytes 1179648 | tf_op jit(solution)/shard_map/psum | solution.py:346
  793.4 13.3 %slice-start = ((s8[6782976]{0:T(1024)(128)(4,1)}), s8[2588672]{0:T(1024)(128)(4,1)S(1)}, s32[]{:S(2)}) async-start(s8[6782976]{0:T(1024)(128)(4,1)} %bitcast.265), calls=%async_computation.18 | async-start | bytes 5177344
  810.9 236.5 %all-reduce.9.cloned.1.call-start = ((), (), s32[]{:S(2)}) async-start(), calls=%async_computation.16 | async-start | bytes 2621440 | tf_op jit(solution)/shard_map/psum | solution.py:342
  823.1 100.0 %copy-start.29 = (f32[3,2,729,16]{2,3,0,1:T(8,128)S(1)}, f32[3,2,729,16]{2,3,0,1:T(8,128)}, u32[]{:S(2)}) copy-start(f32[3,2,729,16]{2,3,0,1:T(8,128)} %copy-done.28) | copy-start | bytes 839812
  823.6 10.1 copy-start.9
  823.6 10.1 copy-start.59
  841.9 12.7 %copy-start.60 = (bf16[2,729,8,72]{1,3,2,0:T(8,128)(2,1)}, bf16[2,729,8,72]{1,3,2,0:T(8,128)(2,1)S(1)}, u32[]{:S(2)}) copy-start(bf16[2,729,8,72]{1,3,2,0:T(8,128)(2,1)S(1)} %bitcast_dynamic-update-slice_fusion.11) | copy-start | bytes 5038852 | tf_op jit(solution)/shard_map/while
  854.5 13.3 %copy-start.6 = (bf16[2,729,8,72]{1,3,2,0:T(8,128)(2,1)S(1)}, bf16[2,729,8,72]{1,3,2,0:T(8,128)(2,1)}, u32[]{:S(2)}) copy-start(bf16[2,729,8,72]{1,3,2,0:T(8,128)(2,1)} %get-tuple-element.353) | copy-start | bytes 5038852 | tf_op jit(solution)/shard_map/while
  854.5 13.3 %copy-start.62 = (bf16[2,729,8,72]{1,3,2,0:T(8,128)(2,1)S(1)}, bf16[2,729,8,72]{1,3,2,0:T(8,128)(2,1)}, u32[]{:S(2)}) copy-start(bf16[2,729,8,72]{1,3,2,0:T(8,128)(2,1)} %get-tuple-element.340) | copy-start | bytes 5038852 | tf_op jit(solution)/shard_map/while
  873.5 10.1 copy-start.9
  873.5 10.1 copy-start.59
  891.7 12.5 %copy-start.60 = (bf16[2,729,8,72]{1,3,2,0:T(8,128)(2,1)}, bf16[2,729,8,72]{1,3,2,0:T(8,128)(2,1)S(1)}, u32[]{:S(2)}) copy-start(bf16[2,729,8,72]{1,3,2,0:T(8,128)(2,1)S(1)} %bitcast_dynamic-update-slice_fusion.11) | copy-start | bytes 5038852 | tf_op jit(solution)/shard_map/while
  904.2 13.2 %copy-start.6 = (bf16[2,729,8,72]{1,3,2,0:T(8,128)(2,1)S(1)}, bf16[2,729,8,72]{1,3,2,0:T(8,128)(2,1)}, u32[]{:S(2)}) copy-start(bf16[2,729,8,72]{1,3,2,0:T(8,128)(2,1)} %get-tuple-element.353) | copy-start | bytes 5038852 | tf_op jit(solution)/shard_map/while
  904.2 13.2 %copy-start.62 = (bf16[2,729,8,72]{1,3,2,0:T(8,128)(2,1)S(1)}, bf16[2,729,8,72]{1,3,2,0:T(8,128)(2,1)}, u32[]{:S(2)}) copy-start(bf16[2,729,8,72]{1,3,2,0:T(8,128)(2,1)} %get-tuple-element.340) | copy-start | bytes 5038852 | tf_op jit(solution)/shard_map/while
  923.1 9.1 copy-start.27
  932.2 262.1 %all-reduce.7.cloned.1.call-start = ((), (), s32[]{:S(2)}) async-start(), calls=%async_computation.15 | async-start | bytes 7077888 | tf_op jit(solution)/shard_map/psum | solution.py:338
  943.4 12.0 copy-start.12
  943.4 263.6 %reduce-scatter.11.cloned.1.call-start = ((), (), s32[]{:S(2)}) async-start(), calls=%async_computation.14 | async-start | bytes 5087232 | tf_op jit(solution)/shard_map/reduce_scatter | solution.py:313
  1194.3 12.7 %copy-start.46 = (f32[729]{0:T(1024)S(1)}, f32[729]{0:T(1024)}, u32[]{:S(2)}) copy-start(f32[729]{0:T(1024)} %copy-done.45) | copy-start | bytes 8752
  1194.3 12.7 %copy-start.49 = (f32[1152]{0:T(1024)S(1)}, f32[1152]{0:T(1024)}, u32[]{:S(2)}) copy-start(f32[1152]{0:T(1024)} %param.28) | copy-start | bytes 13828
  1194.3 12.7 %copy-start.52 = (f32[729]{0:T(1024)S(1)}, f32[729]{0:T(1024)}, u32[]{:S(2)}) copy-start(f32[729]{0:T(1024)} %copy-done.51) | copy-start | bytes 8752
  (48 other events, 214.0 us)
Sparse Core Ops, SparseCore 0:
  18.0 15.1 all-gather.9
  35.0 55.7 all-gather.11
  92.7 30.1 all-gather.13
  178.6 11.1 reduce-scatter.4
  784.6 12.9 all-gather.21
  811.0 55.6 all-reduce.10
  932.3 115.0 all-reduce.8
  1054.5 139.7 all-reduce.6
  1196.7 10.2 reduce-scatter.10
Sparse Core Ops, SparseCore 1:
  182.0 123.2 all-gather.19
  306.9 37.9 all-gather.17
  346.4 123.2 all-gather.15
  539.6 116.8 reduce-scatter.8
  659.0 119.1 reduce-scatter.6
